TPU v7x, 256 devices: a whole 4x4x8 slice. The times are simulated.
256 devices in a mesh: bus: 32 (over x, z), case: 8 (over y, core).
Axes of the slice: x: 4, y: 4, z: 8, core: 2. Of those that a mesh axis runs over, the one named last changes fastest.
Arguments:
- z_columns: float32 [32768, 1024], P('bus')
- resident_bus: int32 [1024], replicated, may hold values from 0 to 32767, as said below
- fault_col: int32 [4096], P('case'), may hold values from 0 to 1023
- switch_cols: int32 [4096, 2], P('case'), may hold values from 0 to 1023, as said below
- tie_x: float32 [4096], P('case'), may hold values from 0.5 to 2
- fault_z: float32 [4096], P('case'), may hold values from 0.5 to 2
- boundary_send: int32 [32, 2, 128], replicated, may hold values from 0 to 1023, as said below
- branch_ends: int32 [49152, 2], P('bus'), may hold values from 0 to 1279, as said below
- branch_x: float32 [49152], P('bus'), may hold values from 0.01 to 0.05
- pickup: float32 [49152], P('bus'), may hold values from 0.2 to 1.5
- tds: float32 [49152], P('bus'), may hold values from 0.05 to 0.5
- curve: int32 [49152], P('bus'), may hold values from 0 to 2
Outputs:
- voltage: float32 [32768, 4096], P('bus', 'case')
- relay_rate: float32 [49152, 4096], P('bus', 'case')
- worst_rate: float32 [49152], P('bus')
Inputs may be any that keep to these rules, and one draw needn't show every extreme that they name: `resident_bus`: distinct bus ids. `switch_cols`: the two columns of a case differ. `boundary_send`: rows sent to the lower block lie among the first 256 rows, rows sent to the upper block among the last 256; each block's live slots come first and hold distinct rows, padding repeats the first slot's row; the first block sends nothing down and the last nothing up; some block fills all 128 slots. `branch_ends`: a to slot of 1024 or more points at a live slot of the neighbour's block; the first block never uses the lower slots, the last never the upper ones; a local to row differs from the from row.
All inputs are finite; a program needn't handle non-finite values.
Results may differ from a plain program's by a relative error of at most 0.000049.
Values sent between devices are 32-bit elements; how exact they have to be, the bound alone decides.
A program may use at most 64 MiB of HBM per device.

v0:
```python
import jax
import jax.numpy as jnp
from jax import lax
from jax.sharding import PartitionSpec as P


def shifted(value, axis, by):
    size = lax.axis_size(axis)
    pairs = [(i, i + by) for i in range(size) if 0 <= i + by < size]
    return lax.ppermute(value, axis, pairs)


def relay_of(currents, pickup, tds, curve):
    factor = jnp.where(curve == 0, 0.14, jnp.where(curve == 1, 13.5, 80.0)).astype(jnp.float32)
    exponent = jnp.where(curve == 0, 0.02, jnp.where(curve == 1, 1.0, 2.0)).astype(jnp.float32)
    scaled = currents / pickup[:, None]
    powered = jnp.exp(0.5 * exponent[:, None] * jnp.log(scaled * scaled + 0.0001))
    return jnp.maximum(powered - 1.0, 0.0) / (factor * tds)[:, None]


def per_device(
    z_columns,
    resident_bus,
    fault_col,
    switch_cols,
    tie_x,
    fault_z,
    boundary_send,
    branch_ends,
    branch_x,
    pickup,
    tds,
    curve,
):
    rows_dev = z_columns.shape[0]
    my_index = lax.axis_index("bus")
    fault_cols = jnp.take(z_columns, fault_col, axis=1)
    branch_diff = jnp.take(z_columns, switch_cols[:, 0], axis=1) - jnp.take(
        z_columns, switch_cols[:, 1], axis=1
    )
    offset = my_index * rows_dev
    row_a = jnp.take(resident_bus, switch_cols[:, 0]) - offset
    row_b = jnp.take(resident_bus, switch_cols[:, 1]) - offset
    row_f = jnp.take(resident_bus, fault_col) - offset
    row_ids = lax.broadcasted_iota(jnp.int32, (rows_dev, 1), 0)

    def pick_rows(column, wanted):
        return jnp.sum(jnp.where(row_ids == wanted[None, :], column, 0.0), axis=0)

    partial_value = jnp.stack(
        [
            pick_rows(branch_diff, row_a) - pick_rows(branch_diff, row_b),
            pick_rows(branch_diff, row_f),
            pick_rows(fault_cols, row_f),
        ]
    )
    own_lists = lax.dynamic_index_in_dim(boundary_send, my_index, 0, keepdims=False)
    entry_sums = lax.psum(partial_value, "bus")
    weight_ratio = entry_sums[1] / (tie_x + entry_sums[0])
    self_z = entry_sums[2] - entry_sums[1] * weight_ratio
    fault_amps = 1.0 / (self_z + fault_z)
    voltage = 1.0 - (fault_cols - branch_diff * weight_ratio[None, :]) * fault_amps[None, :]
    fields = voltage[None]
    going_down = jnp.take(fields, own_lists[0], axis=1)
    going_up = jnp.take(fields, own_lists[1], axis=1)
    from_lower = shifted(going_up, "bus", 1)
    from_upper = shifted(going_down, "bus", -1)
    extended = jnp.concatenate([fields, from_lower, from_upper], axis=1)[0]
    drops = jnp.take(extended, branch_ends[:, 0], axis=0) - jnp.take(
        extended, branch_ends[:, 1], axis=0
    )
    currents = drops / branch_x[:, None]
    relay_rate = relay_of(currents, pickup, tds, curve)
    worst_rate = lax.pmax(jnp.max(relay_rate, axis=1), "case")
    return (voltage, relay_rate, worst_rate)


def solution(mesh):
    in_specs = (
        P("bus", None),
        P(),
        P("case"),
        P("case", None),
        P("case"),
        P("case"),
        P(),
        P("bus", None),
        P("bus"),
        P("bus"),
        P("bus"),
        P("bus"),
    )
    out_specs = (P("bus", "case"), P("bus", "case"), P("bus"))
    return jax.shard_map(
        per_device, mesh=mesh, in_specs=in_specs, out_specs=out_specs, check_vma=False
    )
```

profile of v0, /device:TPU:1, one launch (start us, length us, event | category | flops | bytes accessed | tf_op | source)
XLA Modules:
  0.0 166.8 jit_solution(13267739268833994264)
XLA Ops:
  0.7 0.8 fusion.11
  1.5 3.4 %gather_fusion.4 = s32[512]{0:T(512)S(1)} fusion(s32[1024]{0:T(1024)} %param.21, s32[1024]{0:T(1024)S(1)} %pad_clamp_fusion.4), kind=kCustom, calls=%fused_computation.6.clone | custom fusion | bytes 6144 | tf_op jit(solution)/shard_map/jit(_take)/gather | solution.py:43
  4.8 2.3 %gather_fusion.3 = s32[512]{0:T(512)S(1)} fusion(s32[1024]{0:T(1024)S(1)} %copy-done.1, s32[1024]{0:T(1024)S(1)} %pad_clamp_fusion.5), kind=kCustom, calls=%fused_computation.1.clone | custom fusion | bytes 6144 | tf_op jit(solution)/shard_map/jit(_take)/gather | solution.py:42
  7.1 5.4 %copy.25 = f32[1024,1024]{0,1:T(8,128)} copy(f32[1024,1024]{1,0:T(8,128)} %param.20) | data formatting | bytes 8388608 | tf_op args[0]
  12.5 5.8 %gather_fusion.1 = f32[512,1024]{1,0:T(8,128)} fusion(f32[1024,1024]{0,1:T(8,128)} %copy.25, s32[1024]{0:T(1024)S(1)} %pad_clamp_fusion.5), kind=kCustom, calls=%fused_computation.4.clone | custom fusion | bytes 4196352 | tf_op jit(solution)/shard_map/jit(_take)/gather | solution.py:38
  18.3 5.8 %gather_fusion.2 = f32[512,1024]{1,0:T(8,128)} fusion(f32[1024,1024]{0,1:T(8,128)} %copy.25, s32[1024]{0:T(1024)S(1)} %pad_clamp_fusion.4), kind=kCustom, calls=%fused_computation.5.clone | custom fusion | bytes 4196352 | tf_op jit(solution)/shard_map/jit(_take)/gather | solution.py:38
  24.1 2.3 %gather_fusion.5 = s32[512]{0:T(512)S(1)} fusion(s32[1024]{0:T(1024)S(1)} %copy-done.1, s32[1024]{0:T(1024)S(1)} %pad_clamp_fusion.6), kind=kCustom, calls=%fused_computation.7.clone | custom fusion | bytes 6144 | tf_op jit(solution)/shard_map/jit(_take)/gather | solution.py:44
  26.4 5.0 %gather_fusion = f32[512,1024]{1,0:T(8,128)S(1)} fusion(f32[1024,1024]{0,1:T(8,128)} %copy.25, s32[1024]{0:T(1024)S(1)} %pad_clamp_fusion.6), kind=kCustom, calls=%fused_computation.clone | custom fusion | bytes 4196352 | tf_op jit(solution)/shard_map/jit(_take)/gather | solution.py:37
  31.5 4.2 %select_reduce_fusion.1 = (f32[512]{0:T(512)S(1)}, f32[512]{0:T(512)S(1)}, f32[512]{0:T(512)S(1)}, f32[512]{0:T(512)S(1)}, f32[1024,512]{0,1:T(8,128)}) fusion(s32[512]{0:T(512)S(1)} %get-tuple-element.44, s32[512]{0:T(512)S(1)} %get-tuple-element.33, s32[512]{0:T(512)S(1)} %get-tuple-element.31, f32[512,1024]{1,0:T(8,128)S(1)} %gather_fusion, ...), kind=kLoop, calls=%fused_computation.27 | loop fusion | flops 7862272 | bytes 8404480 | tf_op jit(solution)/shard_map/reduce_sum | solution.py:48
  35.7 65.3 %psum.7 = f32[3,512]{1,0:T(4,128)S(1)} all-reduce(f32[3,512]{1,0:T(4,128)S(1)} %pad_maximum_fusion), channel_id=1, replica_groups=mesh['bus'=32,'case'=8] {'bus'}, use_global_device_ids=true, to_apply=%region_4.7 | all-reduce | flops 1536 | bytes 12288 | tf_op jit(solution)/shard_map/psum | solution.py:58
  101.1 3.4 %fusion.8 = f32[1024,512]{0,1:T(8,128)} fusion(f32[1024,512]{0,1:T(8,128)} %get-tuple-element.30, f32[512,1024]{1,0:T(8,128)S(1)} %gather_fusion, f32[512]{0:T(512)S(1)} %get-tuple-element.28, f32[512]{0:T(512)S(1)} %get-tuple-element.29, pred[512]{0:T(512)(128)(4,1)S(1)} %get-tuple-element.34), kind=kLoop, calls=%fused_computation.24 | loop fusion | flops 2621440 | bytes 6296064 | tf_op jit(solution)/shard_map/sub | solution.py:62
  104.5 1.9 %copy.34 = f32[1024,512]{1,0:T(8,128)S(1)} copy(f32[1024,512]{0,1:T(8,128)} %fusion.8) | data formatting | bytes 4194304
  106.5 0.8 gather_fusion.6
  107.5 1.3 collective-permute-start
  108.8 0.8 gather_fusion.7
  109.7 1.3 collective-permute-start.1
  111.2 0.9 collective-permute-done
  112.2 4.7 %collective-permute-done.1 = f32[1,128,512]{1,2,0:T(8,128)S(1)} collective-permute-done((f32[1,128,512]{1,2,0:T(8,128)S(1)}, f32[1,128,512]{1,2,0:T(8,128)S(1)}, u32[]{:S(2)}, u32[]{:S(2)}) %collective-permute-start.1) | collective-permute-done | bytes 262176 | tf_op jit(solution)/shard_map/ppermute | solution.py:10
  116.9 3.3 %maximum_bitcast_fusion = f32[1280,512]{0,1:T(8,128)} fusion(f32[1,128,512]{1,2,0:T(8,128)S(1)} %collective-permute-done.1, f32[1,128,512]{1,2,0:T(8,128)S(1)} %collective-permute-done, f32[1,1024,512]{1,2,0:T(8,128)} %bitcast.36), kind=kLoop, calls=%fused_computation.18 | loop fusion | flops 1310720 | bytes 5242880 | tf_op jit(solution)/shard_map/squeeze | solution.py:68
  120.2 2.1 %copy.32 = f32[1280,512]{1,0:T(8,128)S(1)} copy(f32[1280,512]{0,1:T(8,128)} %maximum_bitcast_fusion) | data formatting | bytes 5242880 | tf_op jit(solution)/shard_map/squeeze | solution.py:68
  122.3 5.0 %gather_fusion.8 = f32[1536,512]{1,0:T(8,128)} fusion(f32[1280,512]{1,0:T(8,128)S(1)} %copy.32, s32[2048]{0:T(1024)S(1)} %pad_clamp_fusion.1), kind=kCustom, calls=%fused_computation.3.clone | custom fusion | bytes 6297600 | tf_op jit(solution)/shard_map/jit(_take)/gather | solution.py:69
  127.3 4.9 %gather_fusion.9 = f32[1536,512]{1,0:T(8,128)} fusion(f32[1280,512]{1,0:T(8,128)S(1)} %copy.32, s32[2048]{0:T(1024)S(1)} %pad_clamp_fusion), kind=kCustom, calls=%fused_computation.9.clone | custom fusion | bytes 6297600 | tf_op jit(solution)/shard_map/jit(_take)/gather | solution.py:69
  132.2 5.9 %fusion.9 = (f32[1536]{0:T(1024)S(1)}, f32[1536,512]{1,0:T(8,128)}) fusion(f32[1536]{0:T(1024)S(1)} %select_multiply_fusion, f32[1536]{0:T(1024)S(1)} %multiply.4, f32[1536,512]{1,0:T(8,128)} %gather_fusion.9, pred[1536]{0:T(1024)(128)(4,1)S(1)} %get-tuple-element.48, f32[1536,512]{1,0:T(8,128)} %gather_fusion.8, pred[1536]{0:T(1024)(128)(4,1)S(1)} %get-tuple-element.49, ...), kind=kLoop, calls=%fused_computation.67 | loop fusion | flops 8649216 | bytes 9464832 | tf_op jit(solution)/shard_map/reduce_max | solution.py:74
  138.1 28.7 %pmax.7 = f32[1536]{0:T(1024)} all-reduce(f32[1536]{0:T(1024)S(1)} %get-tuple-element.19), channel_id=1, replica_groups=mesh['bus'=32,'case'=8] {'case'}, use_global_device_ids=true, to_apply=%region_6.11 | all-reduce | flops 1536 | bytes 12288 | tf_op jit(solution)/shard_map/pmax | solution.py:74
  (50 shorter events, 0.6 us)
Async XLA Ops:
  0.6 105.8 %copy-start = (s32[32,2,128]{2,1,0:T(2,128)S(1)}, s32[32,2,128]{2,1,0:T(2,128)}, u32[]{:S(2)}) copy-start(s32[32,2,128]{2,1,0:T(2,128)} %param.26) | copy-start | bytes 98308
  0.6 4.2 %copy-start.1 = (s32[1024]{0:T(1024)S(1)}, s32[1024]{0:T(1024)}, u32[]{:S(2)}) copy-start(s32[1024]{0:T(1024)} %param.21) | copy-start | bytes 12292
  18.3 5.8 %copy-start.6 = (s32[512]{0:T(512)S(1)}, s32[512]{0:T(512)}, u32[]{:S(2)}) copy-start(s32[512]{0:T(512)} %param.22) | copy-start | bytes 6148
  31.5 69.6 %copy-start.9 = (f32[512]{0:T(512)S(1)}, f32[512]{0:T(512)}, u32[]{:S(2)}) copy-start(f32[512]{0:T(512)} %param.25) | copy-start | bytes 6148
  31.5 69.6 %copy-start.10 = (f32[512]{0:T(512)S(1)}, f32[512]{0:T(512)}, u32[]{:S(2)}) copy-start(f32[512]{0:T(512)} %param.24) | copy-start | bytes 6148
  106.4 3.1 %copy-start.2 = (f32[1024,512]{1,0:T(8,128)}, f32[1024,512]{1,0:T(8,128)S(1)}, u32[]{:S(2)}) copy-start(f32[1024,512]{1,0:T(8,128)S(1)} %copy.34) | copy-start | bytes 6291460
  107.4 3.6 %copy-start.3 = (s32[1536,2]{0,1:T(2,128)S(1)}, s32[1536,2]{0,1:T(2,128)}, u32[]{:S(2)}) copy-start(s32[1536,2]{0,1:T(2,128)} %param.27) | copy-start | bytes 36868
  107.4 3.7 %copy-start.7 = (s32[1536]{0:T(1024)S(1)}, s32[1536]{0:T(1024)}, u32[]{:S(2)}) copy-start(s32[1536]{0:T(1024)} %param.31) | copy-start | bytes 18436
  107.4 3.8 %copy-start.4 = (f32[1536]{0:T(1024)S(1)}, f32[1536]{0:T(1024)}, u32[]{:S(2)}) copy-start(f32[1536]{0:T(1024)} %param.28) | copy-start | bytes 18436
  107.4 3.8 %copy-start.5 = (f32[1536]{0:T(1024)S(1)}, f32[1536]{0:T(1024)}, u32[]{:S(2)}) copy-start(f32[1536]{0:T(1024)} %param.29) | copy-start | bytes 18436
  107.5 3.8 %copy-start.8 = (f32[1536]{0:T(1024)S(1)}, f32[1536]{0:T(1024)}, u32[]{:S(2)}) copy-start(f32[1536]{0:T(1024)} %param.30) | copy-start | bytes 18436
  107.5 4.7 %collective-permute-start = (f32[1,128,512]{1,2,0:T(8,128)S(1)}, f32[1,128,512]{1,2,0:T(8,128)S(1)}, u32[]{:S(2)}, u32[]{:S(2)}) collective-permute-start(f32[1,128,512]{1,2,0:T(8,128)S(1)} %bitcast_select_fusion.2), channel_id=1, source_target_pairs={{0,8},{8,16},{16,24},{24,32},{32,40},{40,48},{48,56},{56,64},{64,7... | collective-permute-start | bytes 786440 | tf_op jit(solution)/shard_map/ppermute | solution.py:10
  109.7 7.1 %collective-permute-start.1 = (f32[1,128,512]{1,2,0:T(8,128)S(1)}, f32[1,128,512]{1,2,0:T(8,128)S(1)}, u32[]{:S(2)}, u32[]{:S(2)}) collective-permute-start(f32[1,128,512]{1,2,0:T(8,128)S(1)} %bitcast_select_fusion.1), channel_id=1, source_target_pairs={{8,0},{16,8},{24,16},{32,24},{40,32},{48,40},{56,48},{64,56},{72,6... | collective-permute-start | bytes 786440 | tf_op jit(solution)/shard_map/ppermute | solution.py:10
where the time goes:
time: 167 us
  blocking collectives  94.1 us (56%)
  local copies, waits for them, and re-layouts  46.5 us (28%)
  other arithmetic  17 us (10%)
  waiting for transfers between devices  5.62 us (3%)
  starting transfers between devices  2.6 us (2%)
    psum x1, blocking collectives, per_device(): entry_sums = lax.psum(partial_value, 'bus')  65.3 us
    pmax x1, blocking collectives, per_device(): worst_rate = lax.pmax(jnp.max(relay_rate, axis=1), 'case')  28.7 us
    unnamed x24, local copies, waits for them, and re-layouts  7.35 us
    reduce_max x1, other arithmetic, per_device(): worst_rate = lax.pmax(jnp.max(relay_rate, axis=1), 'case')  5.9 us
    gather x1, local copies, waits for them, and re-layouts, per_device(): jnp.take(z_columns, switch_cols[:, 1], axis=1)  5.8 us
    gather x1, local copies, waits for them, and re-layouts, per_device(): jnp.take(z_columns, switch_cols[:, 0], axis=1)  5.78 us
    ppermute x2, waiting for transfers between devices, shifted(): return lax.ppermute(value, axis, pairs)  5.62 us
    gather x1, local copies, waits for them, and re-layouts, per_device(): fault_cols = jnp.take(z_columns, fault_col, axis=1)  5.01 us
  transfers between devices with their start and end apart: 2, of which 2 were waited for; matrix products, arithmetic and copies ran while one was open for 1% of the time, Pallas kernels for 0%

commit v1 on v0

--- a/solution.py
+++ b/solution.py
@@ -55,7 +55,8 @@
         ]
     )
     own_lists = lax.dynamic_index_in_dim(boundary_send, my_index, 0, keepdims=False)
-    entry_sums = lax.psum(partial_value, "bus")
+    terms = lax.all_gather(partial_value, "bus")
+    entry_sums = jnp.sum(terms, axis=0)
     weight_ratio = entry_sums[1] / (tie_x + entry_sums[0])
     self_z = entry_sums[2] - entry_sums[1] * weight_ratio
     fault_amps = 1.0 / (self_z + fault_z)

time: 167 us -> 143 us (0.86)
  blocking collectives: 94.1 us -> 68.1 us
    psum x1 -> x0, blocking collectives: 65.3 us -> none  [per_device(): entry_sums = lax.psum(partial_value, 'bus')]
    all_gather x0 -> x1, blocking collectives: none -> 40.8 us  [per_device(): terms = lax.all_gather(partial_value, 'bus')]
where the time goes in v1:
time: 143 us; the launch traced here: 142 us
  blocking collectives  68.1 us (48%)
  local copies, waits for them, and re-layouts  46.5 us (33%)
  other arithmetic  17.1 us (12%)
  waiting for transfers between devices  5.62 us (4%)
  starting transfers between devices  3.84 us (3%)
    all_gather x1, blocking collectives, per_device(): terms = lax.all_gather(partial_value, 'bus')  40.8 us
    pmax x1, blocking collectives, per_device(): worst_rate = lax.pmax(jnp.max(relay_rate, axis=1), 'case')  27.3 us
    unnamed x24, local copies, waits for them, and re-layouts  7.35 us
    reduce_max x1, other arithmetic, per_device(): worst_rate = lax.pmax(jnp.max(relay_rate, axis=1), 'case')  5.9 us
    gather x1, local copies, waits for them, and re-layouts, per_device(): jnp.take(z_columns, switch_cols[:, 1], axis=1)  5.8 us
    gather x1, local copies, waits for them, and re-layouts, per_device(): jnp.take(z_columns, switch_cols[:, 0], axis=1)  5.78 us
    ppermute x2, waiting for transfers between devices, shifted(): return lax.ppermute(value, axis, pairs)  5.62 us
    gather x1, local copies, waits for them, and re-layouts, per_device(): fault_cols = jnp.take(z_columns, fault_col, axis=1)  5.01 us
  transfers between devices with their start and end apart: 2, of which 2 were waited for; matrix products, arithmetic and copies ran while one was open for 1% of the time, Pallas kernels for 0%

profile of v1, /device:TPU:1, one launch (start us, length us, event | category | flops | bytes accessed | tf_op | source)
XLA Modules:
  0.0 142.2 jit_solution(4963782477146650624)
XLA Ops:
  0.7 0.8 fusion.11
  1.5 3.4 %gather_fusion.4 = s32[512]{0:T(512)S(1)} fusion(s32[1024]{0:T(1024)} %param.21, s32[1024]{0:T(1024)S(1)} %pad_clamp_fusion.4), kind=kCustom, calls=%fused_computation.6.clone | custom fusion | bytes 6144 | tf_op jit(solution)/shard_map/jit(_take)/gather | solution.py:43
  4.8 2.3 %gather_fusion.3 = s32[512]{0:T(512)S(1)} fusion(s32[1024]{0:T(1024)S(1)} %copy-done.1, s32[1024]{0:T(1024)S(1)} %pad_clamp_fusion.5), kind=kCustom, calls=%fused_computation.1.clone | custom fusion | bytes 6144 | tf_op jit(solution)/shard_map/jit(_take)/gather | solution.py:42
  7.1 5.4 %copy.35 = f32[1024,1024]{0,1:T(8,128)} copy(f32[1024,1024]{1,0:T(8,128)} %param.20) | data formatting | bytes 8388608 | tf_op args[0]
  12.5 5.8 %gather_fusion.1 = f32[512,1024]{1,0:T(8,128)} fusion(f32[1024,1024]{0,1:T(8,128)} %copy.35, s32[1024]{0:T(1024)S(1)} %pad_clamp_fusion.5), kind=kCustom, calls=%fused_computation.4.clone | custom fusion | bytes 4196352 | tf_op jit(solution)/shard_map/jit(_take)/gather | solution.py:38
  18.3 5.8 %gather_fusion.2 = f32[512,1024]{1,0:T(8,128)} fusion(f32[1024,1024]{0,1:T(8,128)} %copy.35, s32[1024]{0:T(1024)S(1)} %pad_clamp_fusion.4), kind=kCustom, calls=%fused_computation.5.clone | custom fusion | bytes 4196352 | tf_op jit(solution)/shard_map/jit(_take)/gather | solution.py:38
  24.1 2.3 %gather_fusion.5 = s32[512]{0:T(512)S(1)} fusion(s32[1024]{0:T(1024)S(1)} %copy-done.1, s32[1024]{0:T(1024)S(1)} %pad_clamp_fusion.6), kind=kCustom, calls=%fused_computation.7.clone | custom fusion | bytes 6144 | tf_op jit(solution)/shard_map/jit(_take)/gather | solution.py:44
  26.4 5.0 %gather_fusion = f32[512,1024]{1,0:T(8,128)S(1)} fusion(f32[1024,1024]{0,1:T(8,128)} %copy.35, s32[1024]{0:T(1024)S(1)} %pad_clamp_fusion.6), kind=kCustom, calls=%fused_computation.clone | custom fusion | bytes 4196352 | tf_op jit(solution)/shard_map/jit(_take)/gather | solution.py:37
  31.5 4.2 %select_reduce_fusion.1 = (f32[512]{0:T(512)S(1)}, f32[512]{0:T(512)S(1)}, f32[512]{0:T(512)S(1)}, f32[512]{0:T(512)S(1)}, f32[1024,512]{0,1:T(8,128)}) fusion(s32[512]{0:T(512)S(1)} %get-tuple-element.47, s32[512]{0:T(512)S(1)} %get-tuple-element.36, s32[512]{0:T(512)S(1)} %get-tuple-element.34, f32[512,1024]{1,0:T(8,128)S(1)} %gather_fusion, ...), kind=kLoop, calls=%fused_computation.27 | loop fusion | flops 7862272 | bytes 8404480 | tf_op jit(solution)/shard_map/reduce_sum | solution.py:48
  35.7 40.8 %all-gather.1 = f32[32,3,512]{2,1,0:T(4,128)S(1)} all-gather(f32[1,3,512]{2,1,0:T(4,128)S(1)} %maximum_bitcast_fusion.1), channel_id=2, replica_groups=mesh['bus'=32,'case'=8] {'bus'}, dimensions={0}, use_global_device_ids=true | all-gather | bytes 202752 | tf_op jit(solution)/shard_map/all_gather | solution.py:58
  76.7 3.4 %fusion.8 = f32[1024,512]{0,1:T(8,128)} fusion(f32[1024,512]{0,1:T(8,128)} %get-tuple-element.33, f32[512,1024]{1,0:T(8,128)S(1)} %gather_fusion, f32[512]{0:T(512)S(1)} %get-tuple-element.31, f32[512]{0:T(512)S(1)} %get-tuple-element.32, pred[512]{0:T(512)(128)(4,1)S(1)} %get-tuple-element.37), kind=kLoop, calls=%fused_computation.24 | loop fusion | flops 2621440 | bytes 6296064 | tf_op jit(solution)/shard_map/sub | solution.py:63
  80.1 1.9 %copy.44 = f32[1024,512]{1,0:T(8,128)S(1)} copy(f32[1024,512]{0,1:T(8,128)} %fusion.8) | data formatting | bytes 4194304
  82.1 0.8 gather_fusion.6
  83.1 2.5 %collective-permute-start = (f32[1,128,512]{1,2,0:T(8,128)S(1)}, f32[1,128,512]{1,2,0:T(8,128)S(1)}, u32[]{:S(2)}, u32[]{:S(2)}) collective-permute-start(f32[1,128,512]{1,2,0:T(8,128)S(1)} %bitcast_select_fusion.2), channel_id=1, source_target_pairs={{0,8},{8,16},{16,24},{24,32},{32,40},{40,48},{48,56},{56,64},{64,7... | collective-permute-start | bytes 786440 | tf_op jit(solution)/shard_map/ppermute | solution.py:10
  85.6 0.8 gather_fusion.7
  86.6 1.3 collective-permute-start.1
  88.1 0.9 collective-permute-done
  89.0 4.7 %collective-permute-done.1 = f32[1,128,512]{1,2,0:T(8,128)S(1)} collective-permute-done((f32[1,128,512]{1,2,0:T(8,128)S(1)}, f32[1,128,512]{1,2,0:T(8,128)S(1)}, u32[]{:S(2)}, u32[]{:S(2)}) %collective-permute-start.1) | collective-permute-done | bytes 262176 | tf_op jit(solution)/shard_map/ppermute | solution.py:10
  93.7 3.3 %maximum_bitcast_fusion = f32[1280,512]{0,1:T(8,128)} fusion(f32[1,128,512]{1,2,0:T(8,128)S(1)} %collective-permute-done.1, f32[1,128,512]{1,2,0:T(8,128)S(1)} %collective-permute-done, f32[1,1024,512]{1,2,0:T(8,128)} %bitcast.38), kind=kLoop, calls=%fused_computation.18 | loop fusion | flops 1310720 | bytes 5242880 | tf_op jit(solution)/shard_map/squeeze | solution.py:69
  97.0 2.1 %copy.42 = f32[1280,512]{1,0:T(8,128)S(1)} copy(f32[1280,512]{0,1:T(8,128)} %maximum_bitcast_fusion) | data formatting | bytes 5242880 | tf_op jit(solution)/shard_map/squeeze | solution.py:69
  99.1 5.0 %gather_fusion.8 = f32[1536,512]{1,0:T(8,128)} fusion(f32[1280,512]{1,0:T(8,128)S(1)} %copy.42, s32[2048]{0:T(1024)S(1)} %pad_clamp_fusion.1), kind=kCustom, calls=%fused_computation.3.clone | custom fusion | bytes 6297600 | tf_op jit(solution)/shard_map/jit(_take)/gather | solution.py:70
  104.1 4.9 %gather_fusion.9 = f32[1536,512]{1,0:T(8,128)} fusion(f32[1280,512]{1,0:T(8,128)S(1)} %copy.42, s32[2048]{0:T(1024)S(1)} %pad_clamp_fusion), kind=kCustom, calls=%fused_computation.9.clone | custom fusion | bytes 6297600 | tf_op jit(solution)/shard_map/jit(_take)/gather | solution.py:70
  109.0 5.9 %fusion.9 = (f32[1536]{0:T(1024)S(1)}, f32[1536,512]{1,0:T(8,128)}) fusion(f32[1536]{0:T(1024)S(1)} %select_multiply_fusion, f32[1536]{0:T(1024)S(1)} %multiply.4, f32[1536,512]{1,0:T(8,128)} %gather_fusion.9, pred[1536]{0:T(1024)(128)(4,1)S(1)} %get-tuple-element.51, f32[1536,512]{1,0:T(8,128)} %gather_fusion.8, pred[1536]{0:T(1024)(128)(4,1)S(1)} %get-tuple-element.52, ...), kind=kLoop, calls=%fused_computation.67 | loop fusion | flops 8649216 | bytes 9464832 | tf_op jit(solution)/shard_map/reduce_max | solution.py:75
  114.9 27.3 %pmax.7 = f32[1536]{0:T(1024)} all-reduce(f32[1536]{0:T(1024)S(1)} %get-tuple-element.22), channel_id=1, replica_groups=mesh['bus'=32,'case'=8] {'case'}, use_global_device_ids=true, to_apply=%region_6.11 | all-reduce | flops 1536 | bytes 12288 | tf_op jit(solution)/shard_map/pmax | solution.py:75
  (51 shorter events, 0.6 us)
Async XLA Ops:
  0.6 81.4 %copy-start = (s32[32,2,128]{2,1,0:T(2,128)S(1)}, s32[32,2,128]{2,1,0:T(2,128)}, u32[]{:S(2)}) copy-start(s32[32,2,128]{2,1,0:T(2,128)} %param.26) | copy-start | bytes 98308
  0.6 4.2 %copy-start.1 = (s32[1024]{0:T(1024)S(1)}, s32[1024]{0:T(1024)}, u32[]{:S(2)}) copy-start(s32[1024]{0:T(1024)} %param.21) | copy-start | bytes 12292
  18.3 5.8 %copy-start.6 = (s32[512]{0:T(512)S(1)}, s32[512]{0:T(512)}, u32[]{:S(2)}) copy-start(s32[512]{0:T(512)} %param.22) | copy-start | bytes 6148
  31.5 45.2 %copy-start.9 = (f32[512]{0:T(512)S(1)}, f32[512]{0:T(512)}, u32[]{:S(2)}) copy-start(f32[512]{0:T(512)} %param.25) | copy-start | bytes 6148
  31.5 45.2 %copy-start.10 = (f32[512]{0:T(512)S(1)}, f32[512]{0:T(512)}, u32[]{:S(2)}) copy-start(f32[512]{0:T(512)} %param.24) | copy-start | bytes 6148
  82.0 4.4 %copy-start.2 = (f32[1024,512]{1,0:T(8,128)}, f32[1024,512]{1,0:T(8,128)S(1)}, u32[]{:S(2)}) copy-start(f32[1024,512]{1,0:T(8,128)S(1)} %copy.44) | copy-start | bytes 6291460
  83.0 4.9 %copy-start.3 = (s32[1536,2]{0,1:T(2,128)S(1)}, s32[1536,2]{0,1:T(2,128)}, u32[]{:S(2)}) copy-start(s32[1536,2]{0,1:T(2,128)} %param.27) | copy-start | bytes 36868
  83.0 5.0 %copy-start.7 = (s32[1536]{0:T(1024)S(1)}, s32[1536]{0:T(1024)}, u32[]{:S(2)}) copy-start(s32[1536]{0:T(1024)} %param.31) | copy-start | bytes 18436
  83.0 5.0 %copy-start.4 = (f32[1536]{0:T(1024)S(1)}, f32[1536]{0:T(1024)}, u32[]{:S(2)}) copy-start(f32[1536]{0:T(1024)} %param.28) | copy-start | bytes 18436
  83.0 5.0 %copy-start.5 = (f32[1536]{0:T(1024)S(1)}, f32[1536]{0:T(1024)}, u32[]{:S(2)}) copy-start(f32[1536]{0:T(1024)} %param.29) | copy-start | bytes 18436
  83.0 5.0 %copy-start.8 = (f32[1536]{0:T(1024)S(1)}, f32[1536]{0:T(1024)}, u32[]{:S(2)}) copy-start(f32[1536]{0:T(1024)} %param.30) | copy-start | bytes 18436
  83.1 5.9 %collective-permute-start = (f32[1,128,512]{1,2,0:T(8,128)S(1)}, f32[1,128,512]{1,2,0:T(8,128)S(1)}, u32[]{:S(2)}, u32[]{:S(2)}) collective-permute-start(f32[1,128,512]{1,2,0:T(8,128)S(1)} %bitcast_select_fusion.2), channel_id=1, source_target_pairs={{0,8},{8,16},{16,24},{24,32},{32,40},{40,48},{48,56},{56,64},{64,7... | collective-permute-start | bytes 786440 | tf_op jit(solution)/shard_map/ppermute | solution.py:10
  86.6 7.1 %collective-permute-start.1 = (f32[1,128,512]{1,2,0:T(8,128)S(1)}, f32[1,128,512]{1,2,0:T(8,128)S(1)}, u32[]{:S(2)}, u32[]{:S(2)}) collective-permute-start(f32[1,128,512]{1,2,0:T(8,128)S(1)} %bitcast_select_fusion.1), channel_id=1, source_target_pairs={{8,0},{16,8},{24,16},{32,24},{40,32},{48,40},{56,48},{64,56},{72,6... | collective-permute-start | bytes 786440 | tf_op jit(solution)/shard_map/ppermute | solution.py:10
